TPU v7x, 32 devices: a whole 2x2x4 slice. The times are simulated.
32 devices in a mesh: slab: 4 (over y, x), block: 8 (over z, core).
Axes of the slice: x: 2, y: 2, z: 4, core: 2. Of those that a mesh axis runs over, the one named last changes fastest.
Arguments:
- lanczos_vector: float32 [3, 32, 64, 256], P(None, 'slab', 'block'), may hold values from -200 to 200
- previous_vector: float32 [3, 32, 64, 256], P(None, 'slab', 'block'), may hold values from -30 to 30
- previous_beta: float32 [], replicated, may hold values from 0.3 to 1
- locked_vectors: float32 [16, 3, 32, 64, 256], P(None, None, 'slab', 'block'), may hold values from -0.0039867997 to 0.0039867997
- occupancy: int32 [4, 8, 32], P('slab', 'block'), may hold values 0 or 1
- young: float32 [32, 64, 256], P('slab', 'block'), may hold values from 0.5 to 4
- couplings: float32 [13, 3, 3], replicated, may hold values from -1 to 1, as said below
- coarse_inverse: float32 [96, 96], P(('slab', 'block')), may hold values from -45 to 165, as said below
Outputs:
- remainder: float32 [3, 32, 64, 256], P(None, 'slab', 'block')
- coefficients: float32 [2], replicated
- projections: float32 [16], replicated
Inputs may be any that keep to these rules, and one draw needn't show every extreme that they name: `couplings`: each block is symmetric and positive definite, with positive diagonal larger than the sum of its off-diagonal magnitudes. `coarse_inverse`: symmetric and positive definite.
All inputs are finite; a program needn't handle non-finite values. No bound on the sum of `occupancy` on one device may be relied on, other than what follows from the above.
Results may differ from a plain program's by a relative error of at most 0.0003.
Values sent between devices are 32-bit elements; how exact they have to be, the bound alone decides.
No kernel may reach another device: no remote copies, remote signals or barrier semaphores. Data moves between devices by JAX's collectives and lax.ppermute only.
A program may use at most 128 MiB of HBM per device.

v0:
```python
import jax
import jax.numpy as jnp
from jax import lax
from jax.sharding import PartitionSpec as P

BRICK = 8
ITERS = 3
SHIFT_MASS = 0.02
SMOOTH_WEIGHT = 0.5
VOID_DENSITY = 0.1
HIGHEST_PRECISION = lax.Precision.HIGHEST


def with_halo(block, sides, width):
    for axis, dim in sides:
        count = lax.axis_size(axis)
        forward = [(i, i + 1) for i in range(count - 1)]
        backward = [(target, source) for source, target in forward]
        low = lax.ppermute(
            lax.slice_in_dim(block, block.shape[dim] - width, None, axis=dim), axis, forward
        )
        high = lax.ppermute(lax.slice_in_dim(block, 0, width, axis=dim), axis, backward)
        block = jnp.concatenate([low, block, high], axis=dim)
    return block


def offset_list():
    offsets = []
    for step_x in (-1, 0, 1):
        for step_y in (-1, 0, 1):
            for step_z in (-1, 0, 1):
                offsets.append((step_x, step_y, step_z))
    return offsets


def pair_block(couplings, number):
    if number < 13:
        return couplings[number]
    return couplings[26 - number]


def operate_padded(vector_field, padded_weighted, padded_root, stiffness, root_stiff, couplings):
    span_x, span_y, span_z = (vector_field.shape[1], vector_field.shape[2], vector_field.shape[3])
    accumulate = jnp.zeros_like(vector_field)
    for number, (step_x, step_y, step_z) in enumerate(offset_list()):
        if number == 13:
            continue
        matrix_pair = pair_block(couplings, number)
        root_near = padded_root[
            1 + step_x : 1 + step_x + span_x,
            1 + step_y : 1 + step_y + span_y,
            1 + step_z : 1 + step_z + span_z,
        ]
        weighted_near = padded_weighted[
            :,
            1 + step_x : 1 + step_x + span_x,
            1 + step_y : 1 + step_y + span_y,
            1 + step_z : 1 + step_z + span_z,
        ]
        differ = root_near[None] * vector_field - weighted_near
        for column in range(3):
            accumulate = (
                accumulate + matrix_pair[:, column][:, None, None, None] * differ[column][None]
            )
    return SHIFT_MASS * stiffness[None] * vector_field + root_stiff[None] * accumulate


def diagonal_of(padded_root, stiffness, root_stiff, couplings):
    span_x, span_y, span_z = stiffness.shape
    accumulate = jnp.zeros((3, span_x, span_y, span_z), jnp.float32)
    for number, (step_x, step_y, step_z) in enumerate(offset_list()):
        if number == 13:
            continue
        matrix_pair = pair_block(couplings, number)
        root_near = padded_root[
            1 + step_x : 1 + step_x + span_x,
            1 + step_y : 1 + step_y + span_y,
            1 + step_z : 1 + step_z + span_z,
        ]
        accumulate = accumulate + jnp.diagonal(matrix_pair)[:, None, None, None] * root_near[None]
    return SHIFT_MASS * stiffness[None] + root_stiff[None] * accumulate


def shards(
    lanczos_vector,
    previous_vector,
    previous_beta,
    locked_vectors,
    occupancy,
    young,
    couplings,
    coarse_inverse,
):
    density = jnp.where(occupancy == 1, 1.0, VOID_DENSITY).astype(jnp.float32)
    density = jnp.repeat(jnp.repeat(jnp.repeat(density, BRICK, 0), BRICK, 1), BRICK, 2)
    stiffness = density * young
    root_stiff = jnp.sqrt(stiffness)
    root_edges = with_halo(root_stiff, (("slab", 0), ("block", 1)), 1)
    padded_root = jnp.pad(root_edges, ((0, 0), (0, 0), (1, 1)))
    diagonal = diagonal_of(padded_root, stiffness, root_stiff, couplings)
    span_x, span_y, span_z = stiffness.shape
    slab_count = lax.axis_size("slab")
    block_count = lax.axis_size("block")

    def operate(vector_field):
        edges = with_halo(root_stiff[None] * vector_field, (("slab", 1), ("block", 2)), 1)
        padded_weighted = jnp.pad(edges, ((0, 0), (0, 0), (0, 0), (1, 1)))
        return operate_padded(
            vector_field, padded_weighted, padded_root, stiffness, root_stiff, couplings
        )

    def precondition(residual):
        smooth_first = SMOOTH_WEIGHT * residual / diagonal
        remain = residual - operate(smooth_first)
        block_means = jnp.mean(remain, axis=(1, 2, 3))
        gathered = lax.all_gather(block_means, ("slab", "block"), axis=0, tiled=True)
        own_part = jnp.dot(coarse_inverse, gathered, precision=HIGHEST_PRECISION)
        second = smooth_first + own_part[:, None, None, None]
        leftover = residual - operate(second)
        return second + SMOOTH_WEIGHT * leftover / diagonal

    def paired_sums(residual, smoothed, mapped):
        return lax.psum(
            (jnp.sum(residual * smoothed), jnp.sum(mapped * smoothed)), ("slab", "block")
        )

    solution = jnp.zeros_like(lanczos_vector)
    residual = lanczos_vector
    smoothed = precondition(residual)
    mapped = operate(smoothed)
    gamma_now, delta_now = paired_sums(residual, smoothed, mapped)
    step_size = gamma_now / delta_now
    direction = smoothed
    mapped_dir = mapped
    for number in range(ITERS):
        solution = solution + step_size * direction
        residual = residual - step_size * mapped_dir
        if number + 1 < ITERS:
            smoothed = precondition(residual)
            mapped = operate(smoothed)
            gamma_next, delta_now = paired_sums(residual, smoothed, mapped)
            ratio = gamma_next / gamma_now
            step_size = gamma_next / (delta_now - ratio * gamma_next / step_size)
            direction = smoothed + ratio * direction
            mapped_dir = mapped + ratio * mapped_dir
            gamma_now = gamma_next
    inner_part, weight = lax.psum(
        (jnp.sum(lanczos_vector * solution), jnp.sum(lanczos_vector * lanczos_vector)),
        ("slab", "block"),
    )
    alpha_now = inner_part / weight
    lanczos_part = solution - alpha_now * lanczos_vector - previous_beta * previous_vector
    local_proj = jnp.einsum(
        "kcxyz,cxyz->k", locked_vectors, lanczos_part, precision=HIGHEST_PRECISION
    )
    projections = lax.psum(local_proj, ("slab", "block"))
    remainder = lanczos_part - jnp.einsum(
        "kcxyz,k->cxyz", locked_vectors, projections, precision=HIGHEST_PRECISION
    )
    square = lax.psum(jnp.sum(remainder * remainder), ("slab", "block"))
    cell_count = 3.0 * span_x * span_y * span_z * slab_count * block_count
    beta_norm = jnp.sqrt(square / cell_count)
    return (remainder, jnp.stack([alpha_now, beta_norm]), projections)


def solution(mesh):
    in_specs = (
        P(None, "slab", "block", None),
        P(None, "slab", "block", None),
        P(),
        P(None, None, "slab", "block", None),
        P("slab", "block", None),
        P("slab", "block", None),
        P(),
        P(("slab", "block"), None),
    )
    out_specs = (P(None, "slab", "block", None), P(), P())
    return jax.shard_map(shards, mesh=mesh, in_specs=in_specs, out_specs=out_specs, check_vma=False)
```

profile of v0, /device:TPU:0, one launch (start us, length us, event | category | flops | bytes accessed | tf_op | source)
XLA Modules:
  0.0 647.6 jit_solution(7884673104356321382)
XLA Ops:
  3.8 5.5 collective-permute-start
  9.3 1.4 slice_reduce_fusion.12
  31.5 3.0 collective-permute-start.2
  36.1 2.3 broadcast_multiply_fusion.8
  39.7 5.5 collective-permute-start.4
  48.6 3.6 collective-permute-start.6
  53.3 1.6 select_maximum_fusion.32
  54.9 1.4 slice_subtract_fusion.213
  60.1 1.9 subtract_reduce_fusion.2
  63.8 45.5 %all-reduce.10 = f32[96]{0:T(128)} all-reduce(f32[96]{0:T(128)} %multiply_dynamic-update-slice_fusion.2), channel_id=1, replica_groups=mesh['slab'=4,'block'=8] {'slab','block'}, use_global_device_ids=true, to_apply=%add.10 | all-reduce | flops 96 | bytes 768
  111.6 4.8 collective-permute-start.8
  116.4 1.5 collective-permute-done.8
  119.3 1.5 collective-permute-start.11
  120.8 3.3 collective-permute-done.11
  129.1 1.5 broadcast_multiply_fusion.6
  130.7 1.4 collective-permute-start.13
  132.1 5.4 collective-permute-start.12
  137.6 1.5 collective-permute-done.12
  140.4 4.3 collective-permute-start.14
  147.7 3.2 multiply_reduce_fusion.7
  150.9 45.5 %all-reduce.16 = (f32[]{:T(128)}, f32[]{:T(128)}) all-reduce(f32[]{:T(128)} %get-tuple-element.8, f32[]{:T(128)} %get-tuple-element.7), channel_id=1, replica_groups=mesh['slab'=4,'block'=8] {'slab','block'}, use_global_device_ids=true, to_apply=%region_2.3 | all-reduce | flops 2 | bytes 16 | tf_op jit(solution)/shard_map/psum | solution.py:123
  199.0 1.4 collective-permute-start.17
  200.5 4.8 collective-permute-start.16
  205.3 1.5 collective-permute-done.16
  208.1 3.4 collective-permute-start.18
  212.5 1.4 slice_subtract_fusion.141
  216.6 1.9 subtract_reduce_fusion.1
  220.2 42.9 %all-reduce.11 = f32[96]{0:T(128)} all-reduce(f32[96]{0:T(128)} %multiply_dynamic-update-slice_fusion.1), channel_id=1, replica_groups=mesh['slab'=4,'block'=8] {'slab','block'}, use_global_device_ids=true, to_apply=%add.11 | all-reduce | flops 96 | bytes 768
  265.5 4.8 collective-permute-start.20
  270.3 1.5 collective-permute-done.20
  274.5 3.5 collective-permute-done.23
  278.5 1.3 slice_subtract_fusion.119
  283.0 1.5 broadcast_multiply_fusion.3
  284.7 1.4 collective-permute-start.25
  286.1 5.4 collective-permute-start.24
  291.5 1.5 collective-permute-done.24
  294.4 4.5 collective-permute-start.26
  301.7 3.1 multiply_reduce_fusion.5
  304.8 45.5 %all-reduce.15 = (f32[]{:T(128)}, f32[]{:T(128)}) all-reduce(f32[]{:T(128)} %get-tuple-element.6, f32[]{:T(128)} %get-tuple-element.5), channel_id=1, replica_groups=mesh['slab'=4,'block'=8] {'slab','block'}, use_global_device_ids=true, to_apply=%region_7.8 | all-reduce | flops 2 | bytes 16 | tf_op jit(solution)/shard_map/psum | solution.py:123
  355.9 1.4 collective-permute-start.29
  357.4 4.8 collective-permute-start.28
  362.2 1.5 collective-permute-done.28
  365.0 3.0 collective-permute-start.30
  369.4 1.4 slice_subtract_fusion.69
  373.5 1.9 subtract_reduce_fusion
  377.2 43.0 %all-reduce.12 = f32[96]{0:T(128)} all-reduce(f32[96]{0:T(128)} %multiply_dynamic-update-slice_fusion), channel_id=1, replica_groups=mesh['slab'=4,'block'=8] {'slab','block'}, use_global_device_ids=true, to_apply=%add.12 | all-reduce | flops 96 | bytes 768
  422.5 4.8 collective-permute-start.32
  427.3 1.5 collective-permute-done.32
  430.2 1.5 collective-permute-start.35
  431.7 3.3 collective-permute-done.35
  435.5 1.3 slice_subtract_fusion.47
  440.0 1.5 broadcast_multiply_fusion
  441.7 1.4 collective-permute-start.37
  443.1 5.4 collective-permute-start.36
  448.6 1.5 collective-permute-done.36
  451.4 4.3 collective-permute-start.38
  458.7 2.2 multiply_reduce_fusion.3
  461.5 45.6 %all-reduce.14 = (f32[]{:T(128)}, f32[]{:T(128)}) all-reduce(f32[]{:T(128)} %multiply_reduce_fusion.4, f32[]{:T(128)} %multiply_reduce_fusion.3), channel_id=1, replica_groups=mesh['slab'=4,'block'=8] {'slab','block'}, use_global_device_ids=true, to_apply=%region_12.13 | all-reduce | flops 2 | bytes 16 | tf_op jit(solution)/shard_map/psum | solution.py:123
  510.9 2.5 multiply_reduce_fusion.1
  513.4 40.2 %all-reduce.13 = (f32[]{:T(128)}, f32[]{:T(128)}) all-reduce(f32[]{:T(128)} %get-tuple-element.4, f32[]{:T(128)} %get-tuple-element.3), channel_id=1, replica_groups=mesh['slab'=4,'block'=8] {'slab','block'}, use_global_device_ids=true, to_apply=%region_16.17 | all-reduce | flops 2 | bytes 16 | tf_op jit(solution)/shard_map/psum | solution.py:147
  556.1 5.0 fusion.4
  561.0 40.5 %psum.78 = f32[16]{0:T(128)S(1)} all-reduce(f32[16]{0:T(128)S(1)} %fusion.4), channel_id=1, replica_groups=mesh['slab'=4,'block'=8] {'slab','block'}, use_global_device_ids=true, to_apply=%region_19.20 | all-reduce | flops 16 | bytes 128 | tf_op jit(solution)/shard_map/psum | solution.py:156
  601.6 3.3 fusion
  606.2 39.7 %psum.79 = f32[]{:T(128)} all-reduce(f32[]{:T(128)} %get-tuple-element.69), channel_id=1, replica_groups=mesh['slab'=4,'block'=8] {'slab','block'}, use_global_device_ids=true, to_apply=%region_21.22 | all-reduce | flops 1 | bytes 8 | tf_op jit(solution)/shard_map/psum | solution.py:160
  (1163 shorter events, 86.3 us)
Async XLA Ops:
  0.6 555.4 %copy-start = (f32[16,3,8,8,256]{4,3,2,1,0:T(8,128)S(1)}, f32[16,3,8,8,256]{4,3,2,1,0:T(8,128)}, u32[]{:S(2)}) copy-start(f32[16,3,8,8,256]{4,3,2,1,0:T(8,128)} %param.11) | copy-start | bytes 9437188
  2.5 27.6 %collective-permute-start.1 = (f32[1,8,256]{2,1,0:T(8,128)S(1)}, f32[1,8,256]{2,1,0:T(8,128)S(1)}, u32[]{:S(2)}, u32[]{:S(2)}) collective-permute-start(f32[1,8,256]{2,1,0:T(8,128)S(1)} %get-tuple-element.1154), channel_id=1, source_target_pairs={{8,0},{16,8},{24,16},{9,1},{17,9},{25,17},{10,2},{18,10},{26,18},{... | collective-permute-start | bytes 24584 | tf_op jit(solution)/shard_map/ppermute | solution.py:22
  3.8 26.3 %collective-permute-start = (f32[1,8,256]{2,1,0:T(8,128)S(1)}, f32[1,8,256]{2,1,0:T(8,128)S(1)}, u32[]{:S(2)}, u32[]{:S(2)}) collective-permute-start(f32[1,8,256]{2,1,0:T(8,128)S(1)} %get-tuple-element.1153), channel_id=1, source_target_pairs={{0,8},{8,16},{16,24},{1,9},{9,17},{17,25},{2,10},{10,18},{18,26},{... | collective-permute-start | bytes 24584 | tf_op jit(solution)/shard_map/ppermute | solution.py:19
  30.2 4.4 collective-permute-start.3
  31.5 3.9 collective-permute-start.2
  35.7 17.3 %copy-start.5 = (f32[8,8,256]{2,1,0:T(8,128)}, f32[8,8,256]{2,1,0:T(8,128)S(1)}, u32[]{:S(2)}) copy-start(f32[8,8,256]{2,1,0:T(8,128)S(1)} %get-tuple-element.360) | copy-start | bytes 196612
  35.8 17.2 %copy-start.12 = (f32[8,8,256]{2,1,0:T(8,128)}, f32[8,8,256]{2,1,0:T(8,128)S(1)}, u32[]{:S(2)}) copy-start(f32[8,8,256]{2,1,0:T(8,128)S(1)} %get-tuple-element.361) | copy-start | bytes 196612
  35.8 17.2 %copy-start.19 = (f32[8,8,256]{2,1,0:T(8,128)}, f32[8,8,256]{2,1,0:T(8,128)S(1)}, u32[]{:S(2)}) copy-start(f32[8,8,256]{2,1,0:T(8,128)S(1)} %get-tuple-element.362) | copy-start | bytes 196612
  35.8 17.2 %copy-start.26 = (f32[8,8,256]{2,1,0:T(8,128)}, f32[8,8,256]{2,1,0:T(8,128)S(1)}, u32[]{:S(2)}) copy-start(f32[8,8,256]{2,1,0:T(8,128)S(1)} %get-tuple-element.363) | copy-start | bytes 196612
  35.8 17.2 %copy-start.33 = (f32[8,8,256]{2,1,0:T(8,128)}, f32[8,8,256]{2,1,0:T(8,128)S(1)}, u32[]{:S(2)}) copy-start(f32[8,8,256]{2,1,0:T(8,128)S(1)} %get-tuple-element.364) | copy-start | bytes 196612
  35.8 17.2 %copy-start.40 = (f32[8,8,256]{2,1,0:T(8,128)}, f32[8,8,256]{2,1,0:T(8,128)S(1)}, u32[]{:S(2)}) copy-start(f32[8,8,256]{2,1,0:T(8,128)S(1)} %get-tuple-element.365) | copy-start | bytes 196612
  35.8 17.2 %copy-start.47 = (f32[8,8,256]{2,1,0:T(8,128)}, f32[8,8,256]{2,1,0:T(8,128)S(1)}, u32[]{:S(2)}) copy-start(f32[8,8,256]{2,1,0:T(8,128)S(1)} %get-tuple-element.366) | copy-start | bytes 196612
  35.8 17.2 %copy-start.54 = (f32[8,8,256]{2,1,0:T(8,128)}, f32[8,8,256]{2,1,0:T(8,128)S(1)}, u32[]{:S(2)}) copy-start(f32[8,8,256]{2,1,0:T(8,128)S(1)} %get-tuple-element.367) | copy-start | bytes 196612
  35.8 17.2 %copy-start.61 = (f32[8,8,256]{2,1,0:T(8,128)}, f32[8,8,256]{2,1,0:T(8,128)S(1)}, u32[]{:S(2)}) copy-start(f32[8,8,256]{2,1,0:T(8,128)S(1)} %get-tuple-element.368) | copy-start | bytes 196612
  35.8 17.2 %copy-start.65 = (f32[8,8,256]{2,1,0:T(8,128)}, f32[8,8,256]{2,1,0:T(8,128)S(1)}, u32[]{:S(2)}) copy-start(f32[8,8,256]{2,1,0:T(8,128)S(1)} %get-tuple-element.369) | copy-start | bytes 196612
  35.8 17.2 %copy-start.69 = (f32[8,8,256]{2,1,0:T(8,128)}, f32[8,8,256]{2,1,0:T(8,128)S(1)}, u32[]{:S(2)}) copy-start(f32[8,8,256]{2,1,0:T(8,128)S(1)} %get-tuple-element.370) | copy-start | bytes 196612
  35.9 17.2 %copy-start.73 = (f32[8,8,256]{2,1,0:T(8,128)}, f32[8,8,256]{2,1,0:T(8,128)S(1)}, u32[]{:S(2)}) copy-start(f32[8,8,256]{2,1,0:T(8,128)S(1)} %get-tuple-element.371) | copy-start | bytes 196612
  35.9 17.2 %copy-start.77 = (f32[8,8,256]{2,1,0:T(8,128)}, f32[8,8,256]{2,1,0:T(8,128)S(1)}, u32[]{:S(2)}) copy-start(f32[8,8,256]{2,1,0:T(8,128)S(1)} %get-tuple-element.372) | copy-start | bytes 196612
  35.9 17.2 %copy-start.81 = (f32[8,8,256]{2,1,0:T(8,128)}, f32[8,8,256]{2,1,0:T(8,128)S(1)}, u32[]{:S(2)}) copy-start(f32[8,8,256]{2,1,0:T(8,128)S(1)} %get-tuple-element.373) | copy-start | bytes 196612
  35.9 17.2 %copy-start.85 = (f32[8,8,256]{2,1,0:T(8,128)}, f32[8,8,256]{2,1,0:T(8,128)S(1)}, u32[]{:S(2)}) copy-start(f32[8,8,256]{2,1,0:T(8,128)S(1)} %get-tuple-element.375) | copy-start | bytes 196612
  35.9 17.2 %copy-start.145 = (f32[8,8,256]{2,1,0:T(8,128)}, f32[8,8,256]{2,1,0:T(8,128)S(1)}, u32[]{:S(2)}) copy-start(f32[8,8,256]{2,1,0:T(8,128)S(1)} %get-tuple-element.374) | copy-start | bytes 196612
  35.9 17.2 %copy-start.149 = (f32[8,8,256]{2,1,0:T(8,128)}, f32[8,8,256]{2,1,0:T(8,128)S(1)}, u32[]{:S(2)}) copy-start(f32[8,8,256]{2,1,0:T(8,128)S(1)} %get-tuple-element.376) | copy-start | bytes 196612
  36.0 17.1 %copy-start.103 = (f32[8,8,256]{2,1,0:T(8,128)}, f32[8,8,256]{2,1,0:T(8,128)S(1)}, u32[]{:S(2)}) copy-start(f32[8,8,256]{2,1,0:T(8,128)S(1)} %get-tuple-element.1139) | copy-start | bytes 196612
  36.0 17.1 %copy-start.110 = (f32[8,8,256]{2,1,0:T(8,128)}, f32[8,8,256]{2,1,0:T(8,128)S(1)}, u32[]{:S(2)}) copy-start(f32[8,8,256]{2,1,0:T(8,128)S(1)} %get-tuple-element.1140) | copy-start | bytes 196612
  38.4 7.6 %collective-permute-start.5 = (f32[3,1,8,256]{3,2,1,0:T(8,128)S(1)}, f32[3,1,8,256]{3,2,1,0:T(8,128)S(1)}, u32[]{:S(2)}, u32[]{:S(2)}) collective-permute-start(f32[3,1,8,256]{3,2,1,0:T(8,128)S(1)} %get-tuple-element.1138), channel_id=1, source_target_pairs={{8,0},{16,8},{24,16},{9,1},{17,9},{25,17},{10,2},{18,10},{26,18},{... | collective-permute-start | bytes 73736 | tf_op jit(solution)/shard_map/ppermute | solution.py:22
  39.7 7.0 %collective-permute-start.4 = (f32[3,1,8,256]{3,2,1,0:T(8,128)S(1)}, f32[3,1,8,256]{3,2,1,0:T(8,128)S(1)}, u32[]{:S(2)}, u32[]{:S(2)}) collective-permute-start(f32[3,1,8,256]{3,2,1,0:T(8,128)S(1)} %get-tuple-element.1137), channel_id=1, source_target_pairs={{0,8},{8,16},{16,24},{1,9},{9,17},{17,25},{2,10},{10,18},{18,26},{... | collective-permute-start | bytes 73736 | tf_op jit(solution)/shard_map/ppermute | solution.py:19
  47.3 6.0 collective-permute-start.7
  48.6 4.7 collective-permute-start.6
  110.3 6.1 collective-permute-start.9
  111.6 6.3 collective-permute-start.8
  118.0 2.8 collective-permute-start.10
  119.3 4.8 collective-permute-start.11
  130.7 6.9 %collective-permute-start.13 = (f32[3,1,8,256]{3,2,1,0:T(8,128)S(1)}, f32[3,1,8,256]{3,2,1,0:T(8,128)S(1)}, u32[]{:S(2)}, u32[]{:S(2)}) collective-permute-start(f32[3,1,8,256]{3,2,1,0:T(8,128)S(1)} %get-tuple-element.973), channel_id=1, source_target_pairs={{8,0},{16,8},{24,16},{9,1},{17,9},{25,17},{10,2},{18,10},{26,18},{... | collective-permute-start | bytes 73736 | tf_op jit(solution)/shard_map/ppermute | solution.py:22
  132.1 7.0 %collective-permute-start.12 = (f32[3,1,8,256]{3,2,1,0:T(8,128)S(1)}, f32[3,1,8,256]{3,2,1,0:T(8,128)S(1)}, u32[]{:S(2)}, u32[]{:S(2)}) collective-permute-start(f32[3,1,8,256]{3,2,1,0:T(8,128)S(1)} %get-tuple-element.972), channel_id=1, source_target_pairs={{0,8},{8,16},{16,24},{1,9},{9,17},{17,25},{2,10},{10,18},{18,26},{... | collective-permute-start | bytes 73736 | tf_op jit(solution)/shard_map/ppermute | solution.py:19
  139.1 5.6 collective-permute-start.15
  140.4 5.1 collective-permute-start.14
  198.9 17.3 %copy-start.160 = (f32[3,8,8,256]{3,2,1,0:T(8,128)}, f32[3,8,8,256]{3,2,1,0:T(8,128)S(1)}, u32[]{:S(2)}) copy-start(f32[3,8,8,256]{3,2,1,0:T(8,128)S(1)} %get-tuple-element.82) | copy-start | bytes 589828
  199.0 6.3 collective-permute-start.17
  200.5 6.3 collective-permute-start.16
  206.8 4.7 collective-permute-start.19
  208.1 3.9 collective-permute-start.18
  264.2 6.1 collective-permute-start.21
  265.5 6.3 collective-permute-start.20
  271.9 2.6 collective-permute-start.22
  273.2 4.9 collective-permute-start.23
  284.7 6.9 %collective-permute-start.25 = (f32[3,1,8,256]{3,2,1,0:T(8,128)S(1)}, f32[3,1,8,256]{3,2,1,0:T(8,128)S(1)}, u32[]{:S(2)}, u32[]{:S(2)}) collective-permute-start(f32[3,1,8,256]{3,2,1,0:T(8,128)S(1)} %get-tuple-element.723), channel_id=1, source_target_pairs={{8,0},{16,8},{24,16},{9,1},{17,9},{25,17},{10,2},{18,10},{26,18},{... | collective-permute-start | bytes 73736 | tf_op jit(solution)/shard_map/ppermute | solution.py:22
  286.1 7.0 %collective-permute-start.24 = (f32[3,1,8,256]{3,2,1,0:T(8,128)S(1)}, f32[3,1,8,256]{3,2,1,0:T(8,128)S(1)}, u32[]{:S(2)}, u32[]{:S(2)}) collective-permute-start(f32[3,1,8,256]{3,2,1,0:T(8,128)S(1)} %get-tuple-element.722), channel_id=1, source_target_pairs={{0,8},{8,16},{16,24},{1,9},{9,17},{17,25},{2,10},{10,18},{18,26},{... | collective-permute-start | bytes 73736 | tf_op jit(solution)/shard_map/ppermute | solution.py:19
  293.1 5.8 collective-permute-start.27
  294.4 5.1 collective-permute-start.26
  355.8 17.3 %copy-start.162 = (f32[3,8,8,256]{3,2,1,0:T(8,128)}, f32[3,8,8,256]{3,2,1,0:T(8,128)S(1)}, u32[]{:S(2)}) copy-start(f32[3,8,8,256]{3,2,1,0:T(8,128)S(1)} %get-tuple-element.76) | copy-start | bytes 589828
  355.9 6.3 collective-permute-start.29
  357.4 6.3 collective-permute-start.28
  363.7 4.3 collective-permute-start.31
  365.0 3.9 collective-permute-start.30
  421.2 6.1 collective-permute-start.33
  422.5 6.3 collective-permute-start.32
  428.9 2.8 collective-permute-start.34
  430.2 4.9 collective-permute-start.35
  441.7 6.9 %collective-permute-start.37 = (f32[3,1,8,256]{3,2,1,0:T(8,128)S(1)}, f32[3,1,8,256]{3,2,1,0:T(8,128)S(1)}, u32[]{:S(2)}, u32[]{:S(2)}) collective-permute-start(f32[3,1,8,256]{3,2,1,0:T(8,128)S(1)} %get-tuple-element.473), channel_id=1, source_target_pairs={{8,0},{16,8},{24,16},{9,1},{17,9},{25,17},{10,2},{18,10},{26,18},{... | collective-permute-start | bytes 73736 | tf_op jit(solution)/shard_map/ppermute | solution.py:22
  443.1 7.0 %collective-permute-start.36 = (f32[3,1,8,256]{3,2,1,0:T(8,128)S(1)}, f32[3,1,8,256]{3,2,1,0:T(8,128)S(1)}, u32[]{:S(2)}, u32[]{:S(2)}) collective-permute-start(f32[3,1,8,256]{3,2,1,0:T(8,128)S(1)} %get-tuple-element.472), channel_id=1, source_target_pairs={{0,8},{8,16},{16,24},{1,9},{9,17},{17,25},{2,10},{10,18},{18,26},{... | collective-permute-start | bytes 73736 | tf_op jit(solution)/shard_map/ppermute | solution.py:19
  450.1 6.3 collective-permute-start.39
  451.4 5.1 collective-permute-start.38
  458.6 52.3 %copy-start.4 = (f32[3,8,8,256]{3,2,1,0:T(8,128)S(1)}, f32[3,8,8,256]{3,2,1,0:T(8,128)}, u32[]{:S(2)}) copy-start(f32[3,8,8,256]{3,2,1,0:T(8,128)} %param.8) | copy-start | bytes 589828
  601.6 45.6 %copy-start.386 = (f32[16]{0:T(128)}, f32[16]{0:T(128)S(1)}, u32[]{:S(2)}) copy-start(f32[16]{0:T(128)S(1)} %psum.78) | copy-start | bytes 196
  (363 other events, 1438.8 us)
where the time goes:
time: 658 us; the launch traced here: 648 us
  blocking collectives  388 us (59%)
  starting transfers between devices  108 us (16%)
  other arithmetic  58.5 us (9%)
  local copies, waits for them, and re-layouts  33.5 us (5%)
  waiting for transfers between devices  26.5 us (4%)
  between operations  21.4 us (3%)
  matrix products  11 us (2%)
    psum x3, blocking collectives, paired_sums(): lax.psum((jnp.sum(residual * smoothed), jnp.sum(mapped * smoothed)), ('sl...  137 us
    unnamed x3, blocking collectives  131 us
    ppermute x20, starting transfers between devices, with_halo(): lax.ppermute(lax.slice_in_dim(block, block.shape[dim] - width, None, axis...  81.4 us
    psum x1, blocking collectives, shards(): projections = lax.psum(local_proj, ('slab', 'block'))  40.5 us
    psum x1, blocking collectives, shards(): lax.psum((jnp.sum(lanczos_vector * solution), jnp.sum(lanczos_vector * la...  40.2 us
    psum x1, blocking collectives, shards(): square = lax.psum(jnp.sum(remainder * remainder), ('slab', 'block'))  39.7 us
    ppermute x20, starting transfers between devices, with_halo(): lax.ppermute(lax.slice_in_dim(block, 0, width, axis=dim), axis, backward)  26.9 us
    ppermute x20, waiting for transfers between devices, with_halo(): lax.ppermute(lax.slice_in_dim(block, block.shape[dim] - width, None, axis...  16.3 us
  transfers between devices with their start and end apart: 40, of which 18 were waited for; matrix products, arithmetic and copies ran while one was open for 4% of the time, Pallas kernels for 0%

commit v1 on v0

--- a/solution.py
+++ b/solution.py
@@ -145,8 +145,10 @@
             mapped_dir = mapped + ratio * mapped_dir
             gamma_now = gamma_next
     inner_part, weight = lax.psum(
-        (jnp.sum(lanczos_vector * solution), jnp.sum(lanczos_vector * lanczos_vector)),
-        ("slab", "block"),
+        lax.psum(
+            (jnp.sum(lanczos_vector * solution), jnp.sum(lanczos_vector * lanczos_vector)), "slab"
+        ),
+        "block",
     )
     alpha_now = inner_part / weight
     lanczos_part = solution - alpha_now * lanczos_vector - previous_beta * previous_vector

time: 658 us -> 642 us (0.976)
  blocking collectives: 388 us -> 372 us
    psum x1, blocking collectives: 40.2 us -> 11.2 us  [shards(): lax.psum((jnp.sum(lanczos_vector * solution), jnp.sum(lanczos_vector * la...]
    psum x0 -> x1, blocking collectives: none -> 14.5 us  [shards(): lax.psum(lax.psum((jnp.sum(lanczos_vector * solution), jnp.sum(lanczos_ve...]
where the time goes in v1:
time: 642 us; the launch traced here: 632 us
  blocking collectives  372 us (58%)
  starting transfers between devices  108 us (17%)
  other arithmetic  58.5 us (9%)
  local copies, waits for them, and re-layouts  33.5 us (5%)
  waiting for transfers between devices  26.5 us (4%)
  between operations  21.8 us (3%)
  matrix products  11 us (2%)
    psum x3, blocking collectives, paired_sums(): lax.psum((jnp.sum(residual * smoothed), jnp.sum(mapped * smoothed)), ('sl...  137 us
    unnamed x3, blocking collectives  131 us
    ppermute x20, starting transfers between devices, with_halo(): lax.ppermute(lax.slice_in_dim(block, block.shape[dim] - width, None, axis...  81.4 us
    psum x1, blocking collectives, shards(): square = lax.psum(jnp.sum(remainder * remainder), ('slab', 'block'))  41.6 us
    psum x1, blocking collectives, shards(): projections = lax.psum(local_proj, ('slab', 'block'))  36.8 us
    ppermute x20, starting transfers between devices, with_halo(): lax.ppermute(lax.slice_in_dim(block, 0, width, axis=dim), axis, backward)  26.9 us
    ppermute x20, waiting for transfers between devices, with_halo(): lax.ppermute(lax.slice_in_dim(block, block.shape[dim] - width, None, axis...  16.3 us
    gather x13, local copies, waits for them, and re-layouts, diagonal_of(): jnp.diagonal(matrix_pair)[:, None, None, None] * root_near[None]  15.3 us
  transfers between devices with their start and end apart: 40, of which 18 were waited for; matrix products, arithmetic and copies ran while one was open for 4% of the time, Pallas kernels for 0%

profile of v1, /device:TPU:0, one launch (start us, length us, event | category | flops | bytes accessed | tf_op | source)
XLA Modules:
  0.0 631.7 jit_solution(13906522380621562511)
XLA Ops:
  3.8 5.5 collective-permute-start
  9.3 1.4 slice_reduce_fusion.12
  31.4 3.0 collective-permute-start.2
  36.1 2.3 broadcast_multiply_fusion.8
  39.6 5.5 collective-permute-start.4
  48.6 3.6 collective-permute-start.6
  53.3 1.6 select_maximum_fusion.32
  54.9 1.4 slice_subtract_fusion.213
  60.1 1.9 subtract_reduce_fusion.2
  63.8 45.5 %all-reduce.10 = f32[96]{0:T(128)} all-reduce(f32[96]{0:T(128)} %multiply_dynamic-update-slice_fusion.2), channel_id=1, replica_groups=mesh['slab'=4,'block'=8] {'slab','block'}, use_global_device_ids=true, to_apply=%add.10 | all-reduce | flops 96 | bytes 768
  111.6 4.8 collective-permute-start.8
  116.4 1.5 collective-permute-done.8
  119.2 1.5 collective-permute-start.11
  120.8 3.3 collective-permute-done.11
  129.1 1.5 broadcast_multiply_fusion.6
  130.7 1.4 collective-permute-start.13
  132.1 5.4 collective-permute-start.12
  137.6 1.5 collective-permute-done.12
  140.4 4.3 collective-permute-start.14
  147.7 3.2 multiply_reduce_fusion.7
  150.9 45.5 %all-reduce.15 = (f32[]{:T(128)}, f32[]{:T(128)}) all-reduce(f32[]{:T(128)} %get-tuple-element.8, f32[]{:T(128)} %get-tuple-element.7), channel_id=1, replica_groups=mesh['slab'=4,'block'=8] {'slab','block'}, use_global_device_ids=true, to_apply=%region_2.3 | all-reduce | flops 2 | bytes 16 | tf_op jit(solution)/shard_map/psum | solution.py:123
  199.0 1.4 collective-permute-start.17
  200.5 4.8 collective-permute-start.16
  205.3 1.5 collective-permute-done.16
  208.1 3.4 collective-permute-start.18
  212.5 1.4 slice_subtract_fusion.141
  216.6 1.9 subtract_reduce_fusion.1
  220.3 43.0 %all-reduce.11 = f32[96]{0:T(128)} all-reduce(f32[96]{0:T(128)} %multiply_dynamic-update-slice_fusion.1), channel_id=1, replica_groups=mesh['slab'=4,'block'=8] {'slab','block'}, use_global_device_ids=true, to_apply=%add.11 | all-reduce | flops 96 | bytes 768
  265.6 4.8 collective-permute-start.20
  270.4 1.5 collective-permute-done.20
  274.6 3.5 collective-permute-done.23
  278.6 1.3 slice_subtract_fusion.119
  283.1 1.5 broadcast_multiply_fusion.3
  284.7 1.4 collective-permute-start.25
  286.2 5.4 collective-permute-start.24
  291.6 1.5 collective-permute-done.24
  294.5 4.5 collective-permute-start.26
  301.8 3.1 multiply_reduce_fusion.5
  304.9 45.5 %all-reduce.14 = (f32[]{:T(128)}, f32[]{:T(128)}) all-reduce(f32[]{:T(128)} %get-tuple-element.6, f32[]{:T(128)} %get-tuple-element.5), channel_id=1, replica_groups=mesh['slab'=4,'block'=8] {'slab','block'}, use_global_device_ids=true, to_apply=%region_7.8 | all-reduce | flops 2 | bytes 16 | tf_op jit(solution)/shard_map/psum | solution.py:123
  356.2 1.4 collective-permute-start.29
  357.7 4.8 collective-permute-start.28
  362.5 1.5 collective-permute-done.28
  365.3 3.0 collective-permute-start.30
  369.7 1.4 slice_subtract_fusion.69
  373.8 1.9 subtract_reduce_fusion
  377.5 43.0 %all-reduce.12 = f32[96]{0:T(128)} all-reduce(f32[96]{0:T(128)} %multiply_dynamic-update-slice_fusion), channel_id=1, replica_groups=mesh['slab'=4,'block'=8] {'slab','block'}, use_global_device_ids=true, to_apply=%add.12 | all-reduce | flops 96 | bytes 768
  422.8 4.8 collective-permute-start.32
  427.7 1.5 collective-permute-done.32
  430.5 1.5 collective-permute-start.35
  432.0 3.3 collective-permute-done.35
  440.4 1.5 broadcast_multiply_fusion
  442.0 1.4 collective-permute-start.37
  443.4 5.4 collective-permute-start.36
  448.9 1.5 collective-permute-done.36
  451.7 4.3 collective-permute-start.38
  459.0 2.2 multiply_reduce_fusion.3
  461.8 45.6 %all-reduce.13 = (f32[]{:T(128)}, f32[]{:T(128)}) all-reduce(f32[]{:T(128)} %multiply_reduce_fusion.4, f32[]{:T(128)} %multiply_reduce_fusion.3), channel_id=1, replica_groups=mesh['slab'=4,'block'=8] {'slab','block'}, use_global_device_ids=true, to_apply=%region_12.13 | all-reduce | flops 2 | bytes 16 | tf_op jit(solution)/shard_map/psum | solution.py:123
  511.4 2.5 multiply_reduce_fusion.1
  513.9 11.2 %all-reduce.17 = (f32[]{:T(128)}, f32[]{:T(128)}) all-reduce(f32[]{:T(128)} %get-tuple-element.4, f32[]{:T(128)} %get-tuple-element.3), channel_id=1, replica_groups=mesh['slab'=4,'block'=8] {'slab'}, use_global_device_ids=true, to_apply=%region_16.17 | all-reduce | flops 2 | bytes 16 | tf_op jit(solution)/shard_map/psum | solution.py:148
  525.1 14.5 %all-reduce.16 = (f32[]{:T(128)}, f32[]{:T(128)}) all-reduce(f32[]{:T(128)} %get-tuple-element.69, f32[]{:T(128)} %get-tuple-element.70), channel_id=1, replica_groups=mesh['slab'=4,'block'=8] {'block'}, use_global_device_ids=true, to_apply=%region_17.18 | all-reduce | flops 2 | bytes 16 | tf_op jit(solution)/shard_map/psum | solution.py:147
  541.9 5.0 fusion.4
  546.9 36.8 %psum.94 = f32[16]{0:T(128)S(1)} all-reduce(f32[16]{0:T(128)S(1)} %fusion.4), channel_id=1, replica_groups=mesh['slab'=4,'block'=8] {'slab','block'}, use_global_device_ids=true, to_apply=%region_21.22 | all-reduce | flops 16 | bytes 128 | tf_op jit(solution)/shard_map/psum | solution.py:158
  583.7 3.3 fusion
  588.3 41.6 %psum.95 = f32[]{:T(128)} all-reduce(f32[]{:T(128)} %get-tuple-element.71), channel_id=1, replica_groups=mesh['slab'=4,'block'=8] {'slab','block'}, use_global_device_ids=true, to_apply=%region_23.24 | all-reduce | flops 1 | bytes 8 | tf_op jit(solution)/shard_map/psum | solution.py:162
  (1164 shorter events, 87.7 us)
Async XLA Ops:
  0.6 541.3 %copy-start = (f32[16,3,8,8,256]{4,3,2,1,0:T(8,128)S(1)}, f32[16,3,8,8,256]{4,3,2,1,0:T(8,128)}, u32[]{:S(2)}) copy-start(f32[16,3,8,8,256]{4,3,2,1,0:T(8,128)} %param.11) | copy-start | bytes 9437188
  2.5 27.6 %collective-permute-start.1 = (f32[1,8,256]{2,1,0:T(8,128)S(1)}, f32[1,8,256]{2,1,0:T(8,128)S(1)}, u32[]{:S(2)}, u32[]{:S(2)}) collective-permute-start(f32[1,8,256]{2,1,0:T(8,128)S(1)} %get-tuple-element.1156), channel_id=1, source_target_pairs={{8,0},{16,8},{24,16},{9,1},{17,9},{25,17},{10,2},{18,10},{26,18},{... | collective-permute-start | bytes 24584 | tf_op jit(solution)/shard_map/ppermute | solution.py:22
  3.8 26.3 %collective-permute-start = (f32[1,8,256]{2,1,0:T(8,128)S(1)}, f32[1,8,256]{2,1,0:T(8,128)S(1)}, u32[]{:S(2)}, u32[]{:S(2)}) collective-permute-start(f32[1,8,256]{2,1,0:T(8,128)S(1)} %get-tuple-element.1155), channel_id=1, source_target_pairs={{0,8},{8,16},{16,24},{1,9},{9,17},{17,25},{2,10},{10,18},{18,26},{... | collective-permute-start | bytes 24584 | tf_op jit(solution)/shard_map/ppermute | solution.py:19
  30.1 4.4 collective-permute-start.3
  31.4 3.9 collective-permute-start.2
  35.7 17.3 %copy-start.5 = (f32[8,8,256]{2,1,0:T(8,128)}, f32[8,8,256]{2,1,0:T(8,128)S(1)}, u32[]{:S(2)}) copy-start(f32[8,8,256]{2,1,0:T(8,128)S(1)} %get-tuple-element.362) | copy-start | bytes 196612
  35.7 17.3 %copy-start.12 = (f32[8,8,256]{2,1,0:T(8,128)}, f32[8,8,256]{2,1,0:T(8,128)S(1)}, u32[]{:S(2)}) copy-start(f32[8,8,256]{2,1,0:T(8,128)S(1)} %get-tuple-element.363) | copy-start | bytes 196612
  35.7 17.3 %copy-start.19 = (f32[8,8,256]{2,1,0:T(8,128)}, f32[8,8,256]{2,1,0:T(8,128)S(1)}, u32[]{:S(2)}) copy-start(f32[8,8,256]{2,1,0:T(8,128)S(1)} %get-tuple-element.364) | copy-start | bytes 196612
  35.7 17.3 %copy-start.26 = (f32[8,8,256]{2,1,0:T(8,128)}, f32[8,8,256]{2,1,0:T(8,128)S(1)}, u32[]{:S(2)}) copy-start(f32[8,8,256]{2,1,0:T(8,128)S(1)} %get-tuple-element.365) | copy-start | bytes 196612
  35.7 17.3 %copy-start.33 = (f32[8,8,256]{2,1,0:T(8,128)}, f32[8,8,256]{2,1,0:T(8,128)S(1)}, u32[]{:S(2)}) copy-start(f32[8,8,256]{2,1,0:T(8,128)S(1)} %get-tuple-element.366) | copy-start | bytes 196612
  35.7 17.3 %copy-start.40 = (f32[8,8,256]{2,1,0:T(8,128)}, f32[8,8,256]{2,1,0:T(8,128)S(1)}, u32[]{:S(2)}) copy-start(f32[8,8,256]{2,1,0:T(8,128)S(1)} %get-tuple-element.367) | copy-start | bytes 196612
  35.8 17.3 %copy-start.47 = (f32[8,8,256]{2,1,0:T(8,128)}, f32[8,8,256]{2,1,0:T(8,128)S(1)}, u32[]{:S(2)}) copy-start(f32[8,8,256]{2,1,0:T(8,128)S(1)} %get-tuple-element.368) | copy-start | bytes 196612
  35.8 17.3 %copy-start.54 = (f32[8,8,256]{2,1,0:T(8,128)}, f32[8,8,256]{2,1,0:T(8,128)S(1)}, u32[]{:S(2)}) copy-start(f32[8,8,256]{2,1,0:T(8,128)S(1)} %get-tuple-element.369) | copy-start | bytes 196612
  35.8 17.3 %copy-start.61 = (f32[8,8,256]{2,1,0:T(8,128)}, f32[8,8,256]{2,1,0:T(8,128)S(1)}, u32[]{:S(2)}) copy-start(f32[8,8,256]{2,1,0:T(8,128)S(1)} %get-tuple-element.370) | copy-start | bytes 196612
  35.8 17.3 %copy-start.65 = (f32[8,8,256]{2,1,0:T(8,128)}, f32[8,8,256]{2,1,0:T(8,128)S(1)}, u32[]{:S(2)}) copy-start(f32[8,8,256]{2,1,0:T(8,128)S(1)} %get-tuple-element.371) | copy-start | bytes 196612
  35.8 17.3 %copy-start.69 = (f32[8,8,256]{2,1,0:T(8,128)}, f32[8,8,256]{2,1,0:T(8,128)S(1)}, u32[]{:S(2)}) copy-start(f32[8,8,256]{2,1,0:T(8,128)S(1)} %get-tuple-element.372) | copy-start | bytes 196612
  35.8 17.3 %copy-start.73 = (f32[8,8,256]{2,1,0:T(8,128)}, f32[8,8,256]{2,1,0:T(8,128)S(1)}, u32[]{:S(2)}) copy-start(f32[8,8,256]{2,1,0:T(8,128)S(1)} %get-tuple-element.373) | copy-start | bytes 196612
  35.8 17.3 %copy-start.77 = (f32[8,8,256]{2,1,0:T(8,128)}, f32[8,8,256]{2,1,0:T(8,128)S(1)}, u32[]{:S(2)}) copy-start(f32[8,8,256]{2,1,0:T(8,128)S(1)} %get-tuple-element.374) | copy-start | bytes 196612
  35.8 17.3 %copy-start.81 = (f32[8,8,256]{2,1,0:T(8,128)}, f32[8,8,256]{2,1,0:T(8,128)S(1)}, u32[]{:S(2)}) copy-start(f32[8,8,256]{2,1,0:T(8,128)S(1)} %get-tuple-element.375) | copy-start | bytes 196612
  35.8 17.3 %copy-start.85 = (f32[8,8,256]{2,1,0:T(8,128)}, f32[8,8,256]{2,1,0:T(8,128)S(1)}, u32[]{:S(2)}) copy-start(f32[8,8,256]{2,1,0:T(8,128)S(1)} %get-tuple-element.377) | copy-start | bytes 196612
  35.8 17.3 %copy-start.145 = (f32[8,8,256]{2,1,0:T(8,128)}, f32[8,8,256]{2,1,0:T(8,128)S(1)}, u32[]{:S(2)}) copy-start(f32[8,8,256]{2,1,0:T(8,128)S(1)} %get-tuple-element.376) | copy-start | bytes 196612
  35.9 17.3 %copy-start.149 = (f32[8,8,256]{2,1,0:T(8,128)}, f32[8,8,256]{2,1,0:T(8,128)S(1)}, u32[]{:S(2)}) copy-start(f32[8,8,256]{2,1,0:T(8,128)S(1)} %get-tuple-element.378) | copy-start | bytes 196612
  35.9 17.2 %copy-start.103 = (f32[8,8,256]{2,1,0:T(8,128)}, f32[8,8,256]{2,1,0:T(8,128)S(1)}, u32[]{:S(2)}) copy-start(f32[8,8,256]{2,1,0:T(8,128)S(1)} %get-tuple-element.1141) | copy-start | bytes 196612
  36.0 17.2 %copy-start.110 = (f32[8,8,256]{2,1,0:T(8,128)}, f32[8,8,256]{2,1,0:T(8,128)S(1)}, u32[]{:S(2)}) copy-start(f32[8,8,256]{2,1,0:T(8,128)S(1)} %get-tuple-element.1142) | copy-start | bytes 196612
  38.3 7.6 %collective-permute-start.5 = (f32[3,1,8,256]{3,2,1,0:T(8,128)S(1)}, f32[3,1,8,256]{3,2,1,0:T(8,128)S(1)}, u32[]{:S(2)}, u32[]{:S(2)}) collective-permute-start(f32[3,1,8,256]{3,2,1,0:T(8,128)S(1)} %get-tuple-element.1140), channel_id=1, source_target_pairs={{8,0},{16,8},{24,16},{9,1},{17,9},{25,17},{10,2},{18,10},{26,18},{... | collective-permute-start | bytes 73736 | tf_op jit(solution)/shard_map/ppermute | solution.py:22
  39.6 7.0 %collective-permute-start.4 = (f32[3,1,8,256]{3,2,1,0:T(8,128)S(1)}, f32[3,1,8,256]{3,2,1,0:T(8,128)S(1)}, u32[]{:S(2)}, u32[]{:S(2)}) collective-permute-start(f32[3,1,8,256]{3,2,1,0:T(8,128)S(1)} %get-tuple-element.1139), channel_id=1, source_target_pairs={{0,8},{8,16},{16,24},{1,9},{9,17},{17,25},{2,10},{10,18},{18,26},{... | collective-permute-start | bytes 73736 | tf_op jit(solution)/shard_map/ppermute | solution.py:19
  47.3 6.0 collective-permute-start.7
  48.6 4.7 collective-permute-start.6
  110.3 6.1 collective-permute-start.9
  111.6 6.3 collective-permute-start.8
  117.9 2.8 collective-permute-start.10
  119.2 4.8 collective-permute-start.11
  130.7 6.9 %collective-permute-start.13 = (f32[3,1,8,256]{3,2,1,0:T(8,128)S(1)}, f32[3,1,8,256]{3,2,1,0:T(8,128)S(1)}, u32[]{:S(2)}, u32[]{:S(2)}) collective-permute-start(f32[3,1,8,256]{3,2,1,0:T(8,128)S(1)} %get-tuple-element.975), channel_id=1, source_target_pairs={{8,0},{16,8},{24,16},{9,1},{17,9},{25,17},{10,2},{18,10},{26,18},{... | collective-permute-start | bytes 73736 | tf_op jit(solution)/shard_map/ppermute | solution.py:22
  132.1 7.0 %collective-permute-start.12 = (f32[3,1,8,256]{3,2,1,0:T(8,128)S(1)}, f32[3,1,8,256]{3,2,1,0:T(8,128)S(1)}, u32[]{:S(2)}, u32[]{:S(2)}) collective-permute-start(f32[3,1,8,256]{3,2,1,0:T(8,128)S(1)} %get-tuple-element.974), channel_id=1, source_target_pairs={{0,8},{8,16},{16,24},{1,9},{9,17},{17,25},{2,10},{10,18},{18,26},{... | collective-permute-start | bytes 73736 | tf_op jit(solution)/shard_map/ppermute | solution.py:19
  139.1 5.6 collective-permute-start.15
  140.4 5.1 collective-permute-start.14
  198.9 17.3 %copy-start.160 = (f32[3,8,8,256]{3,2,1,0:T(8,128)}, f32[3,8,8,256]{3,2,1,0:T(8,128)S(1)}, u32[]{:S(2)}) copy-start(f32[3,8,8,256]{3,2,1,0:T(8,128)S(1)} %get-tuple-element.84) | copy-start | bytes 589828
  199.0 6.3 collective-permute-start.17
  200.5 6.3 %collective-permute-start.16 = (f32[3,1,8,256]{3,2,1,0:T(8,128)S(1)}, f32[3,1,8,256]{3,2,1,0:T(8,128)S(1)}, u32[]{:S(2)}, u32[]{:S(2)}) collective-permute-start(f32[3,1,8,256]{3,2,1,0:T(8,128)S(1)} %get-tuple-element.889), channel_id=1, source_target_pairs={{0,8},{8,16},{16,24},{1,9},{9,17},{17,25},{2,10},{10,18},{18,26},{... | collective-permute-start | bytes 73736 | tf_op jit(solution)/shard_map/ppermute | solution.py:19
  206.8 4.7 collective-permute-start.19
  208.1 3.9 collective-permute-start.18
  264.3 6.1 collective-permute-start.21
  265.6 6.3 collective-permute-start.20
  272.0 2.6 collective-permute-start.22
  273.3 4.9 collective-permute-start.23
  284.7 6.9 %collective-permute-start.25 = (f32[3,1,8,256]{3,2,1,0:T(8,128)S(1)}, f32[3,1,8,256]{3,2,1,0:T(8,128)S(1)}, u32[]{:S(2)}, u32[]{:S(2)}) collective-permute-start(f32[3,1,8,256]{3,2,1,0:T(8,128)S(1)} %get-tuple-element.725), channel_id=1, source_target_pairs={{8,0},{16,8},{24,16},{9,1},{17,9},{25,17},{10,2},{18,10},{26,18},{... | collective-permute-start | bytes 73736 | tf_op jit(solution)/shard_map/ppermute | solution.py:22
  286.2 7.0 %collective-permute-start.24 = (f32[3,1,8,256]{3,2,1,0:T(8,128)S(1)}, f32[3,1,8,256]{3,2,1,0:T(8,128)S(1)}, u32[]{:S(2)}, u32[]{:S(2)}) collective-permute-start(f32[3,1,8,256]{3,2,1,0:T(8,128)S(1)} %get-tuple-element.724), channel_id=1, source_target_pairs={{0,8},{8,16},{16,24},{1,9},{9,17},{17,25},{2,10},{10,18},{18,26},{... | collective-permute-start | bytes 73736 | tf_op jit(solution)/shard_map/ppermute | solution.py:19
  293.2 5.8 collective-permute-start.27
  294.5 5.1 collective-permute-start.26
  356.1 17.3 %copy-start.162 = (f32[3,8,8,256]{3,2,1,0:T(8,128)}, f32[3,8,8,256]{3,2,1,0:T(8,128)S(1)}, u32[]{:S(2)}) copy-start(f32[3,8,8,256]{3,2,1,0:T(8,128)S(1)} %get-tuple-element.78) | copy-start | bytes 589828
  356.2 6.3 collective-permute-start.29
  357.7 6.3 %collective-permute-start.28 = (f32[3,1,8,256]{3,2,1,0:T(8,128)S(1)}, f32[3,1,8,256]{3,2,1,0:T(8,128)S(1)}, u32[]{:S(2)}, u32[]{:S(2)}) collective-permute-start(f32[3,1,8,256]{3,2,1,0:T(8,128)S(1)} %get-tuple-element.639), channel_id=1, source_target_pairs={{0,8},{8,16},{16,24},{1,9},{9,17},{17,25},{2,10},{10,18},{18,26},{... | collective-permute-start | bytes 73736 | tf_op jit(solution)/shard_map/ppermute | solution.py:19
  364.0 4.3 collective-permute-start.31
  365.3 3.9 collective-permute-start.30
  421.5 6.1 collective-permute-start.33
  422.8 6.3 collective-permute-start.32
  429.2 2.8 collective-permute-start.34
  430.5 4.9 collective-permute-start.35
  442.0 6.9 %collective-permute-start.37 = (f32[3,1,8,256]{3,2,1,0:T(8,128)S(1)}, f32[3,1,8,256]{3,2,1,0:T(8,128)S(1)}, u32[]{:S(2)}, u32[]{:S(2)}) collective-permute-start(f32[3,1,8,256]{3,2,1,0:T(8,128)S(1)} %get-tuple-element.475), channel_id=1, source_target_pairs={{8,0},{16,8},{24,16},{9,1},{17,9},{25,17},{10,2},{18,10},{26,18},{... | collective-permute-start | bytes 73736 | tf_op jit(solution)/shard_map/ppermute | solution.py:22
  443.4 7.0 %collective-permute-start.36 = (f32[3,1,8,256]{3,2,1,0:T(8,128)S(1)}, f32[3,1,8,256]{3,2,1,0:T(8,128)S(1)}, u32[]{:S(2)}, u32[]{:S(2)}) collective-permute-start(f32[3,1,8,256]{3,2,1,0:T(8,128)S(1)} %get-tuple-element.474), channel_id=1, source_target_pairs={{0,8},{8,16},{16,24},{1,9},{9,17},{17,25},{2,10},{10,18},{18,26},{... | collective-permute-start | bytes 73736 | tf_op jit(solution)/shard_map/ppermute | solution.py:19
  450.4 6.3 collective-permute-start.39
  451.7 5.1 collective-permute-start.38
  458.9 52.4 %copy-start.4 = (f32[3,8,8,256]{3,2,1,0:T(8,128)S(1)}, f32[3,8,8,256]{3,2,1,0:T(8,128)}, u32[]{:S(2)}) copy-start(f32[3,8,8,256]{3,2,1,0:T(8,128)} %param.8) | copy-start | bytes 589828
  583.7 47.5 %copy-start.386 = (f32[16]{0:T(128)}, f32[16]{0:T(128)S(1)}, u32[]{:S(2)}) copy-start(f32[16]{0:T(128)S(1)} %psum.94) | copy-start | bytes 196
  (363 other events, 1439.1 us)
